TPU v7x, 256 devices: a whole 4x4x8 slice. The times are simulated.
256 devices in a mesh: cam: 8 (over z), tm: 32 (over x, y, core).
Axes of the slice: x: 4, y: 4, z: 8, core: 2. Of those that a mesh axis runs over, the one named last changes fastest.
Arguments:
- embeds: bfloat16 [8, 4096, 2048], P(None, 'tm', 'cam'), may hold values from -6 to 6
- w_in: bfloat16 [2048, 2304], replicated, may hold values from -0.125 to 0.125
- log_decay: float32 [8, 32, 4096], P('cam', None, 'tm'), may hold values from -1 to 0, as said below
- clip_keep: float32 [32], replicated, may hold values from 0.55 to 0.8
- clip_starts: int32 [8, 3], P('cam'), may hold values from 1 to 4095
- valid_len: int32 [8], P('cam'), may hold values from 2048 to 4096, as said below
- norm_gain: float32 [2048], replicated, may hold values from 0.1 to 1.9
- g_out: bfloat16 [8, 4096, 2048], P('cam', 'tm'), may hold values from -6 to 6
Outputs:
- layer_out: bfloat16 [8, 4096, 2048], P('cam', 'tm')
- d_embeds: bfloat16 [8, 4096, 2048], P(None, 'tm', 'cam')
- d_w_in: float32 [2048, 2304], P(('cam', 'tm'))
Inputs may be any that keep to these rules, and one draw needn't show every extreme that they name: `log_decay`: negative. `valid_len`: some camera's valid length is 4096 in every draw.
All inputs are finite; a program needn't handle non-finite values.
Results may differ from a plain program's by a relative error of at most 0.014.
Values may be sent and summed in bfloat16 or wider, within the bound.
A program may use at most 128 MiB of HBM per device.

v0:
```python
import math
import jax
import jax.numpy as jnp
from jax import lax
from jax.sharding import PartitionSpec as P

D = 2048
H = 32
P_SIZE = 64
N = 128
Q = 128
HP = 2048
epsilon = 1e-05
precise = lax.Precision.HIGHEST


def prefix_states(block_log, state, reverse):
    size = lax.axis_size("tm")
    extra = jnp.broadcast_to(block_log[:, None, None], (H, 8, N))
    packed = jnp.concatenate([state, extra], axis=1)
    mine = lax.all_to_all(packed, "tm", split_axis=0, concat_axis=0, tiled=True)
    logs = mine[:, P_SIZE, 0]
    parts = mine[:, :P_SIZE].reshape(size, P_SIZE * N)
    cum = jnp.cumsum(logs)
    at = jnp.arange(size)
    if reverse:
        reach = at[None, :] > at[:, None]
        gap = (cum - logs)[None, :] - cum[:, None]
    else:
        reach = at[None, :] < at[:, None]
        gap = (cum - logs)[:, None] - cum[None, :]
    factors = jnp.where(reach, jnp.exp(jnp.where(reach, gap, 0.0)), 0.0)
    entered = jnp.dot(factors, parts, precision=precise).astype(jnp.bfloat16)
    entered = entered.reshape(size, P_SIZE, N)
    return lax.all_to_all(entered, "tm", split_axis=0, concat_axis=0, tiled=True).astype(
        jnp.float32
    )


def on_device(embeds, w_in, log_decay, clip_keep, clip_starts, valid_len, norm_gain, g_out):
    n_cam = lax.axis_size("cam")
    n_tm = lax.axis_size("tm")
    t_dev = embeds.shape[1]
    groups = t_dev // Q
    x_rows = lax.all_to_all(embeds, "cam", split_axis=0, concat_axis=2, tiled=True)[0]
    projected = jnp.dot(x_rows, w_in, preferred_element_type=jnp.float32).astype(jnp.bfloat16)
    positions = lax.axis_index("tm") * t_dev + jnp.arange(t_dev, dtype=jnp.int32)
    is_start = jnp.any(positions[:, None] == clip_starts[0][None, :], axis=1)
    log_rates = log_decay[0] + jnp.where(is_start[None, :], jnp.log(clip_keep)[:, None], 0.0)
    valid_rows = (positions < valid_len[0]).astype(jnp.float32)
    proj_float = projected.astype(jnp.float32)
    x_blocks = (proj_float[:, :HP].reshape(t_dev, H, P_SIZE) * valid_rows[:, None, None]).reshape(
        groups, Q, H, P_SIZE
    )
    b_blocks = proj_float[:, HP : HP + N].reshape(groups, Q, N)
    c_blocks = proj_float[:, HP + N :].reshape(groups, Q, N)
    cum_rate = jnp.cumsum(log_rates.reshape(H, groups, Q), axis=2).transpose(1, 0, 2)
    group_log = cum_rate[:, :, -1]
    causal = jnp.arange(Q)[:, None] >= jnp.arange(Q)[None, :]
    gaps = cum_rate[:, :, :, None] - cum_rate[:, :, None, :]
    weights = jnp.where(causal, jnp.exp(jnp.where(causal, gaps, 0.0)), 0.0)
    scores = jnp.einsum("ktn,ksn->kts", c_blocks, b_blocks, precision=precise)
    mixing = weights * scores[:, None]
    y_in = jnp.einsum("khts,kshp->kthp", mixing, x_blocks, precision=precise)
    tail_decay = jnp.exp(group_log[:, :, None] - cum_rate).transpose(0, 2, 1)
    lift_decay = jnp.exp(cum_rate).transpose(0, 2, 1)
    local_state = jnp.einsum(
        "kshp,ksn->khpn", x_blocks * tail_decay[:, :, :, None], b_blocks, precision=precise
    )
    zero_before = [jnp.zeros((H, P_SIZE, N), jnp.float32)]
    zero_end = jnp.exp(group_log[-1])[:, None, None] * zero_before[-1] + local_state[-1]
    block_log = jnp.sum(group_log, axis=0)
    s_in = prefix_states(block_log, zero_end, False)
    lead_log = jnp.cumsum(group_log, axis=0) - group_log
    state_before = jnp.exp(lead_log)[:, :, None, None] * s_in[None] + jnp.stack(zero_before)
    y_out = lift_decay[:, :, :, None] * jnp.einsum(
        "khpn,ktn->kthp", state_before, c_blocks, precision=precise
    )
    raw_out = (y_in + y_out).reshape(t_dev, H, P_SIZE)
    inv_rms = lax.rsqrt(jnp.mean(raw_out * raw_out, axis=-1, keepdims=True) + epsilon)
    normed = raw_out * inv_rms
    layer_out = (normed.reshape(t_dev, HP) * norm_gain[None, :] * valid_rows[:, None]).astype(
        jnp.bfloat16
    )
    d_normed = (g_out[0].astype(jnp.float32) * norm_gain[None, :] * valid_rows[:, None]).reshape(
        t_dev, H, P_SIZE
    )
    d_output = inv_rms * (d_normed - normed * jnp.mean(d_normed * normed, axis=-1, keepdims=True))
    d_blocks = d_output.reshape(groups, Q, H, P_SIZE)
    back_state = jnp.einsum(
        "kthp,ktn->khpn", d_blocks * lift_decay[:, :, :, None], c_blocks, precision=precise
    )
    zero_after = [jnp.zeros((H, P_SIZE, N), jnp.float32)]
    zero_start = jnp.exp(group_log[0])[:, None, None] * zero_after[0] + back_state[0]
    r_out = prefix_states(block_log, zero_start, True)
    trail_log = jnp.cumsum(group_log[::-1], axis=0)[::-1] - group_log
    grad_after = jnp.exp(trail_log)[:, :, None, None] * r_out[None] + jnp.stack(zero_after)
    d_inputs = jnp.einsum("khts,kthp->kshp", mixing, d_blocks, precision=precise)
    d_inputs = d_inputs + tail_decay[:, :, :, None] * jnp.einsum(
        "khpn,ksn->kshp", grad_after, b_blocks, precision=precise
    )
    pair_terms = weights * jnp.einsum("kthp,kshp->khts", d_blocks, x_blocks, precision=precise)
    d_c = jnp.einsum("khts,ksn->ktn", pair_terms, b_blocks, precision=precise)
    d_c = d_c + jnp.einsum(
        "kthp,khpn->ktn", d_blocks * lift_decay[:, :, :, None], state_before, precision=precise
    )
    d_b = jnp.einsum("khts,ktn->ksn", pair_terms, c_blocks, precision=precise)
    d_b = d_b + jnp.einsum(
        "kshp,khpn->ksn", x_blocks * tail_decay[:, :, :, None], grad_after, precision=precise
    )
    du_rows = d_inputs.reshape(t_dev, HP) * valid_rows[:, None]
    d_proj = jnp.concatenate(
        [du_rows, d_b.reshape(t_dev, N), d_c.reshape(t_dev, N)], axis=1
    ).astype(jnp.bfloat16)
    all_proj = lax.all_gather(d_proj, "cam").reshape(n_cam * t_dev, HP + 2 * N)
    width = D // n_cam
    w_mine = lax.dynamic_slice_in_dim(w_in, lax.axis_index("cam") * width, width, axis=0)
    d_embeds = (
        lax.dot_general(
            all_proj, w_mine, (((1,), (1,)), ((), ())), preferred_element_type=jnp.float32
        )
        .astype(jnp.bfloat16)
        .reshape(n_cam, t_dev, width)
    )
    grad_scale = 1.0 / math.sqrt(n_cam * t_dev * n_tm)
    row_terms = grad_scale * lax.dot_general(
        embeds.reshape(n_cam * t_dev, width),
        all_proj,
        (((0,), (0,)), ((), ())),
        preferred_element_type=jnp.float32,
    )
    d_w_in = lax.psum_scatter(row_terms, "tm", scatter_dimension=0, tiled=True)
    return (layer_out[None], d_embeds, d_w_in)


def solution(mesh):
    return jax.shard_map(
        on_device,
        mesh=mesh,
        in_specs=(
            P(None, "tm", "cam"),
            P(),
            P("cam", None, "tm"),
            P(),
            P("cam", None),
            P("cam"),
            P(),
            P("cam", "tm", None),
        ),
        out_specs=(P("cam", "tm", None), P(None, "tm", "cam"), P(("cam", "tm"), None)),
        check_vma=False,
    )
```

profile of v0, /device:TPU:2, one launch (start us, length us, event | category | flops | bytes accessed | tf_op | source)
XLA Modules:
  0.0 300.5 jit_solution(2047633472301824590)
XLA Ops:
  7.2 2.1 copy.62
  9.3 8.5 %all-to-all-start = ((bf16[8,128,256]{1,2,0:T(8,128)(2,1)}), bf16[8,128,256]{1,2,0:T(8,128)(2,1)S(1)}, u32[]{:S(2)}, u32[]{:S(2)}) async-start(bf16[8,128,256]{1,2,0:T(8,128)(2,1)} %copy.62), calls=%async_computation | async-start | bytes 1048576 | tf_op jit(solution)/shard_map/all_to_all | solution.py:45
  19.6 15.6 %all-to-all-done = bf16[8,128,256]{1,2,0:T(8,128)(2,1)S(1)} async-done(((bf16[8,128,256]{1,2,0:T(8,128)(2,1)}), bf16[8,128,256]{1,2,0:T(8,128)(2,1)S(1)}, u32[]{:S(2)}, u32[]{:S(2)}) %all-to-all-start) | async-done | bytes 524320 | tf_op jit(solution)/shard_map/all_to_all | solution.py:45
  35.2 5.1 %convolution_convert_fusion.2 = bf16[128,2304]{1,0:T(8,128)(2,1)S(1)} fusion(bf16[128,2048]{0,1:T(8,128)(2,1)S(1)} %bitcast.133, bf16[2048,2304]{1,0:T(8,128)(2,1)} %param.9), kind=kOutput, calls=%fused_computation.5 | convolution fusion | flops 1208254464 | bytes 10551296 | tf_op jit(solution)/shard_map/dot_general | solution.py:46
  42.7 7.8 %all-to-all-start.1 = ((f32[32,72,128]{2,1,0:T(8,128)}), f32[32,72,128]{2,1,0:T(8,128)}, u32[]{:S(2)}, u32[]{:S(2)}) async-start(f32[32,72,128]{2,1,0:T(8,128)} %pad_maximum_fusion.1), calls=%async_computation.1 | async-start | bytes 2359296 | tf_op jit(solution)/shard_map/all_to_all | solution.py:21
  51.9 14.5 %all-to-all-done.1 = f32[32,72,128]{2,1,0:T(8,128)} async-done(((f32[32,72,128]{2,1,0:T(8,128)}), f32[32,72,128]{2,1,0:T(8,128)}, u32[]{:S(2)}, u32[]{:S(2)}) %all-to-all-start.1) | async-done | bytes 1179680 | tf_op jit(solution)/shard_map/all_to_all | solution.py:21
  71.6 6.9 %all-to-all-start.2 = ((bf16[32,64,128]{2,1,0:T(8,128)(2,1)}), bf16[32,64,128]{2,1,0:T(8,128)(2,1)}, u32[]{:S(2)}, u32[]{:S(2)}) async-start(bf16[32,64,128]{2,1,0:T(8,128)(2,1)} %bitcast.135), calls=%async_computation.2 | async-start | bytes 1048576 | tf_op jit(solution)/shard_map/all_to_all | solution.py:35
  79.6 2.6 copy.63
  82.3 6.5 %fusion.7 = f32[1,128,32,64]{1,3,2,0:T(8,128)} fusion(f32[128,128]{1,0:T(8,128)S(1)} %fusion.65, f32[32,128]{1,0:T(8,128)S(1)} %bitcast.139, pred[128,128]{1,0:T(8,128)(4,1)S(1)} %iota_compare_fusion, f32[128,32,64]{0,2,1:T(8,128)} %bitcast.136, f32[128]{0:T(128)S(1)} %compare_convert_fusion), kind=kOutput, calls=%fused_computation.13 | convolution fusion | flops 405012480 | bytes 2195968 | tf_op jit(solution)/shard_map/khts,kshp->kthp/dot_general | solution.py:64
  88.8 2.2 fusion.32
  95.6 7.5 %all-to-all-start.3 = ((f32[32,72,128]{2,1,0:T(8,128)}), f32[32,72,128]{2,1,0:T(8,128)}, u32[]{:S(2)}, u32[]{:S(2)}) async-start(f32[32,72,128]{2,1,0:T(8,128)} %pad_maximum_fusion), calls=%async_computation.3 | async-start | bytes 2359296 | tf_op jit(solution)/shard_map/all_to_all | solution.py:21
  103.1 5.2 %multiply_reduce_fusion = f32[128,128]{1,0:T(8,128)S(1)} fusion(f32[1,128,32,64]{1,3,2,0:T(8,128)S(1)} %subtract_multiply_fusion, f32[32,128]{1,0:T(8,128)S(1)} %bitcast.140, pred[128,128]{1,0:T(8,128)(4,1)S(1)} %iota_compare_fusion, f32[128,32,64]{0,2,1:T(8,128)} %bitcast.137, f32[128]{0:T(128)S(1)} %compare_convert_fusion), kind=kOutput, calls=%fused_computation.6 | convolution fusion | flops 405520384 | bytes 2195968 | tf_op jit(solution)/shard_map/kthp,kshp->khts/dot_general | solution.py:102
  108.3 10.7 %all-to-all-done.3 = f32[32,72,128]{2,1,0:T(8,128)} async-done(((f32[32,72,128]{2,1,0:T(8,128)}), f32[32,72,128]{2,1,0:T(8,128)}, u32[]{:S(2)}, u32[]{:S(2)}) %all-to-all-start.3) | async-done | bytes 1179680 | tf_op jit(solution)/shard_map/all_to_all | solution.py:21
  124.2 7.1 %all-to-all-start.4 = ((bf16[32,64,128]{2,1,0:T(8,128)(2,1)}), bf16[32,64,128]{2,1,0:T(8,128)(2,1)}, u32[]{:S(2)}, u32[]{:S(2)}) async-start(bf16[32,64,128]{2,1,0:T(8,128)(2,1)} %bitcast.134), calls=%async_computation.4 | async-start | bytes 1048576 | tf_op jit(solution)/shard_map/all_to_all | solution.py:35
  131.4 3.0 convolution_bitcast_fusion.1
  135.3 3.4 %fusion.10 = f32[1,128,32,64]{1,3,2,0:T(8,128)} fusion(f32[1,128,32,64]{1,3,2,0:T(8,128)S(1)} %subtract_multiply_fusion, f32[128,128]{1,0:T(8,128)S(1)} %fusion.65, f32[32,128]{1,0:T(8,128)S(1)} %bitcast.141, pred[128,128]{1,0:T(8,128)(4,1)S(1)} %iota_compare_fusion), kind=kOutput, calls=%fused_computation.14 | convolution fusion | flops 404750336 | bytes 2195456 | tf_op jit(solution)/shard_map/khts,kthp->kshp/dot_general | solution.py:98
  138.7 2.6 all-to-all-done.4
  141.3 2.9 convolution_bitcast_fusion.2
  145.2 1.8 fusion.16
  148.4 53.9 %all-gather.2.cloned.1.call-done = bf16[8,128,2304]{2,1,0:T(8,128)(2,1)} async-done(((bf16[1,128,2304]{2,1,0:T(8,128)(2,1)}), bf16[8,128,2304]{2,1,0:T(8,128)(2,1)}) %all-gather.2.cloned.1.call-update) | async-done | bytes 4718608 | tf_op jit(solution)/shard_map/all_gather | solution.py:115
  202.3 3.9 %fusion.1 = f32[256,2304]{0,1:T(8,128)S(1)} fusion(bf16[8,128,2304]{2,1,0:T(8,128)(2,1)} %all-gather.2.cloned.1.call-done, bf16[8,128,256]{2,1,0:T(8,128)(2,1)} %param.8), kind=kOutput, calls=%fused_computation.4 | convolution fusion | flops 1208549376 | bytes 7602176 | tf_op jit(solution)/shard_map/dot_general | solution.py:126
  206.2 2.0 copy.86
  209.9 4.9 %convolution_convert_fusion.3 = bf16[1024,256]{1,0:T(8,128)(2,1)} fusion(bf16[1024,2304]{1,0:T(8,128)(2,1)} %bitcast.144, bf16[2048,2304]{1,0:T(8,128)(2,1)} %param.9, s32[]{:T(128)S(6)} %select_n.49), kind=kOutput, calls=%fused_computation.23 | convolution fusion | flops 1208221696 | bytes 6422532 | tf_op jit(solution)/shard_map/dot_general | solution.py:119
  214.8 78.9 %reduce-scatter.4.cloned.1.call-done = f32[8,2304]{1,0:T(8,128)} async-done(((f32[256,2304]{1,0:T(8,128)}), f32[8,2304]{1,0:T(8,128)}) %reduce-scatter.4.cloned.1.call-update) | async-done | bytes 73744
  (69 shorter events, 26.2 us)
Async XLA Ops:
  7.2 10.6 %copy-start.5 = (s32[1,3]{1,0:T(1,128)S(1)}, s32[1,3]{1,0:T(1,128)}, u32[]{:S(2)}) copy-start(s32[1,3]{1,0:T(1,128)} %param.12) | copy-start | bytes 40
  7.2 10.6 %copy-start.6 = (f32[32]{0:T(128)S(1)}, f32[32]{0:T(128)}, u32[]{:S(2)}) copy-start(f32[32]{0:T(128)} %param.11) | copy-start | bytes 388
  7.2 11.3 %copy-start.4 = (f32[1,32,128]{2,1,0:T(8,128)S(1)}, f32[1,32,128]{2,1,0:T(8,128)}, u32[]{:S(2)}) copy-start(f32[1,32,128]{2,1,0:T(8,128)} %param.10) | copy-start | bytes 49156
  9.3 26.0 %all-to-all-start = ((bf16[8,128,256]{1,2,0:T(8,128)(2,1)}), bf16[8,128,256]{1,2,0:T(8,128)(2,1)S(1)}, u32[]{:S(2)}, u32[]{:S(2)}) async-start(bf16[8,128,256]{1,2,0:T(8,128)(2,1)} %copy.62), calls=%async_computation | async-start | bytes 1048576 | tf_op jit(solution)/shard_map/all_to_all | solution.py:45
  40.3 41.9 %copy-start.1 = (bf16[128,2304]{1,0:T(8,128)(2,1)}, bf16[128,2304]{1,0:T(8,128)(2,1)S(1)}, u32[]{:S(2)}) copy-start(bf16[128,2304]{1,0:T(8,128)(2,1)S(1)} %convolution_convert_fusion.2) | copy-start | bytes 1769476
  42.7 9.1 %copy-start.3 = (f32[2048]{0:T(1024)S(1)}, f32[2048]{0:T(1024)}, u32[]{:S(2)}) copy-start(f32[2048]{0:T(1024)} %param.14) | copy-start | bytes 24580
  42.7 23.7 %all-to-all-start.1 = ((f32[32,72,128]{2,1,0:T(8,128)}), f32[32,72,128]{2,1,0:T(8,128)}, u32[]{:S(2)}, u32[]{:S(2)}) async-start(f32[32,72,128]{2,1,0:T(8,128)} %pad_maximum_fusion.1), calls=%async_computation.1 | async-start | bytes 2359296 | tf_op jit(solution)/shard_map/all_to_all | solution.py:21
  51.8 39.3 %copy-start = (f32[1,128,2048]{1,2,0:T(8,128)}, f32[1,128,2048]{1,2,0:T(8,128)S(1)}, u32[]{:S(2)}) copy-start(f32[1,128,2048]{1,2,0:T(8,128)S(1)} %copy.69) | copy-start | bytes 3145732
  71.6 17.2 %all-to-all-start.2 = ((bf16[32,64,128]{2,1,0:T(8,128)(2,1)}), bf16[32,64,128]{2,1,0:T(8,128)(2,1)}, u32[]{:S(2)}, u32[]{:S(2)}) async-start(bf16[32,64,128]{2,1,0:T(8,128)(2,1)} %bitcast.135), calls=%async_computation.2 | async-start | bytes 1048576 | tf_op jit(solution)/shard_map/all_to_all | solution.py:35
  95.6 23.4 %all-to-all-start.3 = ((f32[32,72,128]{2,1,0:T(8,128)}), f32[32,72,128]{2,1,0:T(8,128)}, u32[]{:S(2)}, u32[]{:S(2)}) async-start(f32[32,72,128]{2,1,0:T(8,128)} %pad_maximum_fusion), calls=%async_computation.3 | async-start | bytes 2359296 | tf_op jit(solution)/shard_map/all_to_all | solution.py:21
  124.2 17.0 %all-to-all-start.4 = ((bf16[32,64,128]{2,1,0:T(8,128)(2,1)}), bf16[32,64,128]{2,1,0:T(8,128)(2,1)}, u32[]{:S(2)}, u32[]{:S(2)}) async-start(bf16[32,64,128]{2,1,0:T(8,128)(2,1)} %bitcast.134), calls=%async_computation.4 | async-start | bytes 1048576 | tf_op jit(solution)/shard_map/all_to_all | solution.py:35
  131.4 70.9 %all-gather.2.cloned.1.call-start = ((), (), s32[]{:S(2)}) async-start(), calls=%async_computation.6 | async-start | bytes 5308416 | tf_op jit(solution)/shard_map/all_gather | solution.py:115
  138.7 6.5 %copy-start.2 = (f32[1,128,32,64]{1,3,2,0:T(8,128)S(1)}, f32[1,128,32,64]{1,3,2,0:T(8,128)}, u32[]{:S(2)}) copy-start(f32[1,128,32,64]{1,3,2,0:T(8,128)} %fusion.10) | copy-start | bytes 3145732
  148.4 145.3 %reduce-scatter.4.cloned.1.call-start = ((), (), s32[]{:S(2)}) async-start(), calls=%async_computation.7 | async-start | bytes 2433024
Sparse Core Ops, SparseCore 0:
  148.5 53.7 all-gather.1
  208.4 85.3 reduce-scatter.3
where the time goes:
time: 302 us; the launch traced here: 301 us
  waiting for transfers between devices  176 us (58%)
  matrix products  46 us (15%)
  starting transfers between devices  37.9 us (13%)
  local copies, waits for them, and re-layouts  17 us (6%)
  between operations  15.1 us (5%)
  other arithmetic  8.47 us (3%)
    unnamed x3, waiting for transfers between devices  78.9 us
    all_gather x1, waiting for transfers between devices, on_device(): all_proj = lax.all_gather(d_proj, 'cam').reshape(n_cam * t_dev, HP + 2 * N)  53.9 us
    all_to_all x2, waiting for transfers between devices, prefix_states(): mine = lax.all_to_all(packed, 'tm', split_axis=0, concat_axis=0, tiled=True)  25.2 us
    all_to_all x1, waiting for transfers between devices, on_device(): lax.all_to_all(embeds, 'cam', split_axis=0, concat_axis=2, tiled=True)[0]  15.6 us
    all_to_all x2, starting transfers between devices, prefix_states(): mine = lax.all_to_all(packed, 'tm', split_axis=0, concat_axis=0, tiled=True)  15.3 us
    all_to_all x2, starting transfers between devices, prefix_states(): lax.all_to_all(entered, 'tm', split_axis=0, concat_axis=0, tiled=True)  14 us
    all_to_all x1, starting transfers between devices, on_device(): lax.all_to_all(embeds, 'cam', split_axis=0, concat_axis=2, tiled=True)[0]  8.47 us
    dot_general x1, matrix products, on_device(): y_in = jnp.einsum('khts,kshp->kthp', mixing, x_blocks, precision=precise)  6.51 us
  transfers between devices with their start and end apart: 7, of which 6 were waited for; matrix products, arithmetic and copies ran while one was open for 11% of the time, Pallas kernels for 0%

commit v1 on v0

--- a/solution.py
+++ b/solution.py
@@ -42,7 +42,10 @@
     n_tm = lax.axis_size("tm")
     t_dev = embeds.shape[1]
     groups = t_dev // Q
-    x_rows = lax.all_to_all(embeds, "cam", split_axis=0, concat_axis=2, tiled=True)[0]
+    x_rows = jnp.concatenate(
+        lax.all_to_all(jnp.stack(jnp.split(embeds, lax.axis_size("cam"), axis=0)), "cam", 0, 0),
+        axis=2,
+    )[0]
     projected = jnp.dot(x_rows, w_in, preferred_element_type=jnp.float32).astype(jnp.bfloat16)
     positions = lax.axis_index("tm") * t_dev + jnp.arange(t_dev, dtype=jnp.int32)
     is_start = jnp.any(positions[:, None] == clip_starts[0][None, :], axis=1)

time: 302 us -> 307 us (1.017)
  local copies, waits for them, and re-layouts: 17 us -> 22 us
    unnamed x18 -> x32, local copies, waits for them, and re-layouts: 5.9 us -> 9.21 us
  transfers between devices with their start and end apart: 7 -> 7, of which waited for: 6 -> 6; matrix products, arithmetic and copies ran while one was open for 11% -> 10% of each run, Pallas kernels for 0% -> 0%
where the time goes in v1:
time: 307 us; the launch traced here: 306 us
  waiting for transfers between devices  176 us (57%)
  matrix products  46 us (15%)
  starting transfers between devices  37.9 us (12%)
  local copies, waits for them, and re-layouts  22 us (7%)
  between operations  15.1 us (5%)
  other arithmetic  8.47 us (3%)
    unnamed x3, waiting for transfers between devices  78.9 us
    all_gather x1, waiting for transfers between devices, on_device(): all_proj = lax.all_gather(d_proj, 'cam').reshape(n_cam * t_dev, HP + 2 * N)  53.9 us
    all_to_all x2, waiting for transfers between devices, prefix_states(): mine = lax.all_to_all(packed, 'tm', split_axis=0, concat_axis=0, tiled=True)  25.2 us
    all_to_all x1, waiting for transfers between devices, on_device(): lax.all_to_all(jnp.stack(jnp.split(embeds, lax.axis_size('cam'), axis=0))...  15.6 us
    all_to_all x2, starting transfers between devices, prefix_states(): mine = lax.all_to_all(packed, 'tm', split_axis=0, concat_axis=0, tiled=True)  15.3 us
    all_to_all x2, starting transfers between devices, prefix_states(): lax.all_to_all(entered, 'tm', split_axis=0, concat_axis=0, tiled=True)  14 us
    unnamed x32, local copies, waits for them, and re-layouts  9.21 us
    all_to_all x1, starting transfers between devices, on_device(): lax.all_to_all(jnp.stack(jnp.split(embeds, lax.axis_size('cam'), axis=0))...  8.47 us
  transfers between devices with their start and end apart: 7, of which 6 were waited for; matrix products, arithmetic and copies ran while one was open for 10% of the time, Pallas kernels for 0%

profile of v1, /device:TPU:2, one launch (start us, length us, event | category | flops | bytes accessed | tf_op | source)
XLA Modules:
  0.0 305.7 jit_solution(15883910910922309794)
XLA Ops:
  14.4 8.5 %all-to-all-start = ((bf16[8,1,128,256]{2,3,1,0:T(8,128)(2,1)}), bf16[8,1,128,256]{2,3,1,0:T(8,128)(2,1)S(1)}, u32[]{:S(2)}, u32[]{:S(2)}) async-start(bf16[8,1,128,256]{2,3,1,0:T(8,128)(2,1)} %bitcast_dynamic-update-slice_fusion), calls=%async_computation | async-start | bytes 1048576 | tf_op jit(solution)/shard_map/all_to_all | solution.py:46
  24.7 15.6 %all-to-all-done = bf16[8,1,128,256]{2,3,1,0:T(8,128)(2,1)S(1)} async-done(((bf16[8,1,128,256]{2,3,1,0:T(8,128)(2,1)}), bf16[8,1,128,256]{2,3,1,0:T(8,128)(2,1)S(1)}, u32[]{:S(2)}, u32[]{:S(2)}) %all-to-all-start) | async-done | bytes 524320 | tf_op jit(solution)/shard_map/all_to_all | solution.py:46
  40.3 5.1 %convolution_convert_fusion.2 = bf16[128,2304]{1,0:T(8,128)(2,1)S(1)} fusion(bf16[128,2048]{0,1:T(8,128)(2,1)S(1)} %bitcast.149, bf16[2048,2304]{1,0:T(8,128)(2,1)} %param.9), kind=kOutput, calls=%fused_computation.5 | convolution fusion | flops 1208254464 | bytes 10551296 | tf_op jit(solution)/shard_map/dot_general | solution.py:49
  47.8 7.8 %all-to-all-start.1 = ((f32[32,72,128]{2,1,0:T(8,128)}), f32[32,72,128]{2,1,0:T(8,128)}, u32[]{:S(2)}, u32[]{:S(2)}) async-start(f32[32,72,128]{2,1,0:T(8,128)} %pad_maximum_fusion.1), calls=%async_computation.1 | async-start | bytes 2359296 | tf_op jit(solution)/shard_map/all_to_all | solution.py:21
  57.0 14.5 %all-to-all-done.1 = f32[32,72,128]{2,1,0:T(8,128)} async-done(((f32[32,72,128]{2,1,0:T(8,128)}), f32[32,72,128]{2,1,0:T(8,128)}, u32[]{:S(2)}, u32[]{:S(2)}) %all-to-all-start.1) | async-done | bytes 1179680 | tf_op jit(solution)/shard_map/all_to_all | solution.py:21
  74.2 1.6 fusion.17
  76.7 6.9 %all-to-all-start.2 = ((bf16[32,64,128]{2,1,0:T(8,128)(2,1)}), bf16[32,64,128]{2,1,0:T(8,128)(2,1)}, u32[]{:S(2)}, u32[]{:S(2)}) async-start(bf16[32,64,128]{2,1,0:T(8,128)(2,1)} %bitcast.151), calls=%async_computation.2 | async-start | bytes 1048576 | tf_op jit(solution)/shard_map/all_to_all | solution.py:35
  84.8 2.6 copy.86
  87.4 6.5 %fusion.7 = f32[1,128,32,64]{1,3,2,0:T(8,128)} fusion(f32[128,128]{1,0:T(8,128)S(1)} %fusion.65, f32[32,128]{1,0:T(8,128)S(1)} %bitcast.155, pred[128,128]{1,0:T(8,128)(4,1)S(1)} %iota_compare_fusion, f32[128,32,64]{0,2,1:T(8,128)} %bitcast.152, f32[128]{0:T(128)S(1)} %compare_convert_fusion), kind=kOutput, calls=%fused_computation.13 | convolution fusion | flops 405012480 | bytes 2195968 | tf_op jit(solution)/shard_map/khts,kshp->kthp/dot_general | solution.py:67
  94.0 2.2 fusion.32
  100.7 7.5 %all-to-all-start.3 = ((f32[32,72,128]{2,1,0:T(8,128)}), f32[32,72,128]{2,1,0:T(8,128)}, u32[]{:S(2)}, u32[]{:S(2)}) async-start(f32[32,72,128]{2,1,0:T(8,128)} %pad_maximum_fusion), calls=%async_computation.3 | async-start | bytes 2359296 | tf_op jit(solution)/shard_map/all_to_all | solution.py:21
  108.2 5.2 %multiply_reduce_fusion = f32[128,128]{1,0:T(8,128)S(1)} fusion(f32[1,128,32,64]{1,3,2,0:T(8,128)S(1)} %subtract_multiply_fusion, f32[32,128]{1,0:T(8,128)S(1)} %bitcast.156, pred[128,128]{1,0:T(8,128)(4,1)S(1)} %iota_compare_fusion, f32[128,32,64]{0,2,1:T(8,128)} %bitcast.153, f32[128]{0:T(128)S(1)} %compare_convert_fusion), kind=kOutput, calls=%fused_computation.6 | convolution fusion | flops 405520384 | bytes 2195968 | tf_op jit(solution)/shard_map/kthp,kshp->khts/dot_general | solution.py:105
  113.4 10.7 %all-to-all-done.3 = f32[32,72,128]{2,1,0:T(8,128)} async-done(((f32[32,72,128]{2,1,0:T(8,128)}), f32[32,72,128]{2,1,0:T(8,128)}, u32[]{:S(2)}, u32[]{:S(2)}) %all-to-all-start.3) | async-done | bytes 1179680 | tf_op jit(solution)/shard_map/all_to_all | solution.py:21
  129.4 7.1 %all-to-all-start.4 = ((bf16[32,64,128]{2,1,0:T(8,128)(2,1)}), bf16[32,64,128]{2,1,0:T(8,128)(2,1)}, u32[]{:S(2)}, u32[]{:S(2)}) async-start(bf16[32,64,128]{2,1,0:T(8,128)(2,1)} %bitcast.150), calls=%async_computation.4 | async-start | bytes 1048576 | tf_op jit(solution)/shard_map/all_to_all | solution.py:35
  136.5 3.0 convolution_bitcast_fusion.1
  140.5 3.4 %fusion.10 = f32[1,128,32,64]{1,3,2,0:T(8,128)} fusion(f32[1,128,32,64]{1,3,2,0:T(8,128)S(1)} %subtract_multiply_fusion, f32[128,128]{1,0:T(8,128)S(1)} %fusion.65, f32[32,128]{1,0:T(8,128)S(1)} %bitcast.157, pred[128,128]{1,0:T(8,128)(4,1)S(1)} %iota_compare_fusion), kind=kOutput, calls=%fused_computation.14 | convolution fusion | flops 404750336 | bytes 2195456 | tf_op jit(solution)/shard_map/khts,kthp->kshp/dot_general | solution.py:101
  143.8 2.6 all-to-all-done.4
  146.4 2.9 convolution_bitcast_fusion.2
  150.4 1.8 fusion.16
  153.6 53.9 %all-gather.2.cloned.1.call-done = bf16[8,128,2304]{2,1,0:T(8,128)(2,1)} async-done(((bf16[1,128,2304]{2,1,0:T(8,128)(2,1)}), bf16[8,128,2304]{2,1,0:T(8,128)(2,1)}) %all-gather.2.cloned.1.call-update) | async-done | bytes 4718608 | tf_op jit(solution)/shard_map/all_gather | solution.py:118
  207.4 3.9 %fusion.1 = f32[256,2304]{0,1:T(8,128)S(1)} fusion(bf16[8,128,2304]{2,1,0:T(8,128)(2,1)} %all-gather.2.cloned.1.call-done, bf16[8,128,256]{2,1,0:T(8,128)(2,1)} %param.8), kind=kOutput, calls=%fused_computation.4 | convolution fusion | flops 1208549376 | bytes 7602176 | tf_op jit(solution)/shard_map/dot_general | solution.py:129
  211.3 2.0 copy.109
  215.1 4.9 %convolution_convert_fusion.3 = bf16[1024,256]{1,0:T(8,128)(2,1)} fusion(bf16[1024,2304]{1,0:T(8,128)(2,1)} %bitcast.160, bf16[2048,2304]{1,0:T(8,128)(2,1)} %param.9, s32[]{:T(128)S(6)} %select_n.49), kind=kOutput, calls=%fused_computation.23 | convolution fusion | flops 1208221696 | bytes 6422532 | tf_op jit(solution)/shard_map/dot_general | solution.py:122
  219.9 78.9 %reduce-scatter.4.cloned.1.call-done = f32[8,2304]{1,0:T(8,128)} async-done(((f32[256,2304]{1,0:T(8,128)}), f32[8,2304]{1,0:T(8,128)}) %reduce-scatter.4.cloned.1.call-update) | async-done | bytes 73744
  (85 shorter events, 31.7 us)
Async XLA Ops:
  7.2 15.7 %copy-start.5 = (s32[1,3]{1,0:T(1,128)S(1)}, s32[1,3]{1,0:T(1,128)}, u32[]{:S(2)}) copy-start(s32[1,3]{1,0:T(1,128)} %param.12) | copy-start | bytes 40
  7.2 15.8 %copy-start.6 = (f32[32]{0:T(128)S(1)}, f32[32]{0:T(128)}, u32[]{:S(2)}) copy-start(f32[32]{0:T(128)} %param.11) | copy-start | bytes 388
  7.2 16.4 %copy-start.4 = (f32[1,32,128]{2,1,0:T(8,128)S(1)}, f32[1,32,128]{2,1,0:T(8,128)}, u32[]{:S(2)}) copy-start(f32[1,32,128]{2,1,0:T(8,128)} %param.10) | copy-start | bytes 49156
  14.4 26.0 %all-to-all-start = ((bf16[8,1,128,256]{2,3,1,0:T(8,128)(2,1)}), bf16[8,1,128,256]{2,3,1,0:T(8,128)(2,1)S(1)}, u32[]{:S(2)}, u32[]{:S(2)}) async-start(bf16[8,1,128,256]{2,3,1,0:T(8,128)(2,1)} %bitcast_dynamic-update-slice_fusion), calls=%async_computation | async-start | bytes 1048576 | tf_op jit(solution)/shard_map/all_to_all | solution.py:46
  45.4 41.9 %copy-start.1 = (bf16[128,2304]{1,0:T(8,128)(2,1)}, bf16[128,2304]{1,0:T(8,128)(2,1)S(1)}, u32[]{:S(2)}) copy-start(bf16[128,2304]{1,0:T(8,128)(2,1)S(1)} %convolution_convert_fusion.2) | copy-start | bytes 1769476
  47.8 9.1 %copy-start.3 = (f32[2048]{0:T(1024)S(1)}, f32[2048]{0:T(1024)}, u32[]{:S(2)}) copy-start(f32[2048]{0:T(1024)} %param.14) | copy-start | bytes 24580
  47.8 23.7 %all-to-all-start.1 = ((f32[32,72,128]{2,1,0:T(8,128)}), f32[32,72,128]{2,1,0:T(8,128)}, u32[]{:S(2)}, u32[]{:S(2)}) async-start(f32[32,72,128]{2,1,0:T(8,128)} %pad_maximum_fusion.1), calls=%async_computation.1 | async-start | bytes 2359296 | tf_op jit(solution)/shard_map/all_to_all | solution.py:21
  56.9 39.3 %copy-start = (f32[1,128,2048]{1,2,0:T(8,128)}, f32[1,128,2048]{1,2,0:T(8,128)S(1)}, u32[]{:S(2)}) copy-start(f32[1,128,2048]{1,2,0:T(8,128)S(1)} %copy.92) | copy-start | bytes 3145732
  76.7 17.2 %all-to-all-start.2 = ((bf16[32,64,128]{2,1,0:T(8,128)(2,1)}), bf16[32,64,128]{2,1,0:T(8,128)(2,1)}, u32[]{:S(2)}, u32[]{:S(2)}) async-start(bf16[32,64,128]{2,1,0:T(8,128)(2,1)} %bitcast.151), calls=%async_computation.2 | async-start | bytes 1048576 | tf_op jit(solution)/shard_map/all_to_all | solution.py:35
  100.7 23.4 %all-to-all-start.3 = ((f32[32,72,128]{2,1,0:T(8,128)}), f32[32,72,128]{2,1,0:T(8,128)}, u32[]{:S(2)}, u32[]{:S(2)}) async-start(f32[32,72,128]{2,1,0:T(8,128)} %pad_maximum_fusion), calls=%async_computation.3 | async-start | bytes 2359296 | tf_op jit(solution)/shard_map/all_to_all | solution.py:21
  129.4 17.0 %all-to-all-start.4 = ((bf16[32,64,128]{2,1,0:T(8,128)(2,1)}), bf16[32,64,128]{2,1,0:T(8,128)(2,1)}, u32[]{:S(2)}, u32[]{:S(2)}) async-start(bf16[32,64,128]{2,1,0:T(8,128)(2,1)} %bitcast.150), calls=%async_computation.4 | async-start | bytes 1048576 | tf_op jit(solution)/shard_map/all_to_all | solution.py:35
  136.5 70.9 %all-gather.2.cloned.1.call-start = ((), (), s32[]{:S(2)}) async-start(), calls=%async_computation.6 | async-start | bytes 5308416 | tf_op jit(solution)/shard_map/all_gather | solution.py:118
  143.8 6.5 %copy-start.2 = (f32[1,128,32,64]{1,3,2,0:T(8,128)S(1)}, f32[1,128,32,64]{1,3,2,0:T(8,128)}, u32[]{:S(2)}) copy-start(f32[1,128,32,64]{1,3,2,0:T(8,128)} %fusion.10) | copy-start | bytes 3145732
  153.5 145.3 %reduce-scatter.4.cloned.1.call-start = ((), (), s32[]{:S(2)}) async-start(), calls=%async_computation.7 | async-start | bytes 2433024
Sparse Core Ops, SparseCore 0:
  153.6 53.7 all-gather.1
  213.5 85.3 reduce-scatter.3
